TPU v7x, 128 devices: a whole 4x4x4 slice. The times are simulated.
128 devices in a mesh: lag: 16 (over z_lo, x, core), row: 8 (over y, z_hi).
Axes of the slice: x: 4, y: 4, z: 4 (z_hi: 2, z_lo: 2; z = z_hi * 2 + z_lo), core: 2. Of those that a mesh axis runs over, the one named last changes fastest.
Arguments:
- lag_matrix: bfloat16 [16, 8192, 8192], P('lag', 'row'), may hold values from -0.015625 to 0.015625
- past_current: bfloat16 [16, 256, 8192], P('lag', None, 'row'), may hold values from -6 to 6
- excitation: float32 [2, 256, 8192], P(None, None, 'row'), may hold values from -6 to 6
- block_inverse: float32 [64, 128, 128], P('row'), may hold values from -2 to 3
Outputs:
- currents: bfloat16 [2, 256, 8192], P(None, 'lag', 'row')
All inputs are finite; a program needn't handle non-finite values.
Results may differ from a plain program's by a relative error of at most 0.002.
Values may be sent and summed in bfloat16 or wider, within the bound.
A program may use at most 64 MiB of HBM per device.

v0:
```python
import jax
import jax.numpy as jnp
from jax import lax
from jax.sharding import PartitionSpec as P

STEPS = 2


def in_blocks(x, dim, peers):
    before, after = (x.shape[:dim], x.shape[dim + 1 :])
    return jnp.moveaxis(x.reshape(*before, peers, -1, *after), dim, 0)


def summed_on_arrival(x, axis, dim):
    tiles = in_blocks(x, dim, lax.axis_size(axis))
    arrived = lax.all_to_all(tiles, axis, split_axis=0, concat_axis=0, tiled=True)
    return arrived.sum(axis=0)


def in_order(tiles, dim):
    tiles = jnp.moveaxis(tiles, 0, dim)
    lengths = tiles.shape
    return tiles.reshape(*lengths[:dim], lengths[dim] * lengths[dim + 1], *lengths[dim + 2 :])


def from_everyone(x, axis):
    peers = lax.axis_size(axis)
    return lax.all_to_all(jnp.broadcast_to(x[None], (peers, *x.shape)), axis, 0, 0, tiled=True)


def gather_directly(x, axis, dim):
    return in_order(from_everyone(x, axis), dim)


def from_behind(x, axis, by):
    peers = lax.axis_size(axis)
    pairs = [(i, i + by) for i in range(peers) if 0 <= i + by < peers]
    return lax.ppermute(x, axis, pairs)


def solve_blocks(source, block_inverse):
    count = source.shape[0]
    pieces = source.reshape(count, block_inverse.shape[0], block_inverse.shape[1])
    result = jnp.einsum("bij,rbj->rbi", block_inverse, pieces, precision=lax.Precision.HIGHEST)
    return result.reshape(count, source.shape[1]).astype(jnp.bfloat16)


def advance(older, newest, leading):
    incoming_rest = jnp.concatenate([older, leading[:-1]], axis=0)
    first = lax.axis_index("lag") == 0
    head = jnp.where(first, newest[None], incoming_rest)
    return jnp.concatenate([head, incoming_rest[1:]], axis=0)


def per_device(lag_matrix, past_current, excitation, block_inverse):
    lag_count = lax.axis_size("lag")
    excite_all = past_current.shape[1]
    share = excite_all // lag_count
    offset = lax.axis_index("lag") * share
    current_loc = past_current
    results = []
    for step in range(STEPS):
        partial_value = jnp.einsum(
            "lrc,lkc->rk",
            lax.all_gather(current_loc, "row", axis=2, tiled=True),
            lag_matrix,
            preferred_element_type=jnp.float32,
        )
        history = summed_on_arrival(partial_value, "lag", 0)
        mine = lax.dynamic_slice_in_dim(excitation[step], offset, share, 0)
        newest_part = solve_blocks(mine - history, block_inverse)
        results.append(newest_part)
        if step + 1 < STEPS:
            newest = gather_directly(newest_part, "lag", 0)
        if step + 1 < STEPS:
            older = from_behind(current_loc, "lag", 1)
            current_loc = advance(older, newest, current_loc)
    return jnp.stack(results)


def solution(mesh):
    in_specs = (
        P("lag", "row", None),
        P("lag", None, "row"),
        P(None, None, "row"),
        P("row", None, None),
    )
    out_specs = P(None, "lag", "row")
    return jax.shard_map(
        per_device, mesh=mesh, in_specs=in_specs, out_specs=out_specs, check_vma=False
    )
```

profile of v0, /device:TPU:1, one launch (start us, length us, event | category | flops | bytes accessed | tf_op | source)
XLA Modules:
  0.0 246.1 jit_solution(4965949983607384674)
XLA Ops:
  6.5 0.0 copy-start
  6.5 0.7 all-gather.3.cloned.1.call-update
  7.3 76.9 %all-gather.3.cloned.1.call-done = bf16[1,256,8192]{2,1,0:T(8,128)(2,1)} async-done(((bf16[1,256,1024]{2,1,0:T(8,128)(2,1)}), bf16[1,256,8192]{2,1,0:T(8,128)(2,1)}) %all-gather.3.cloned.1.call-update) | async-done | bytes 4194320 | tf_op jit(solution)/shard_map/all_gather | solution.py:65
  84.2 12.6 %fusion.2 = f32[16,16,1024]{2,1,0:T(8,128)} fusion(bf16[16,16,8192]{2,1,0:T(8,128)(2,1)} %bitcast.44, bf16[1,1024,8192]{2,1,0:T(8,128)(2,1)} %param.4), kind=kOutput, calls=%fused_computation.2 | convolution fusion | flops 4294967296 | bytes 22020096 | tf_op jit(solution)/shard_map/lrc,lkc->rk/dot_general | solution.py:63
  96.7 5.4 %all-to-all-start = ((f32[16,16,1024]{2,1,0:T(8,128)}), f32[16,16,1024]{2,1,0:T(8,128)S(1)}, u32[]{:S(2)}, u32[]{:S(2)}) async-start(f32[16,16,1024]{2,1,0:T(8,128)} %fusion.2), calls=%async_computation | async-start | bytes 2097152 | tf_op jit(solution)/shard_map/all_to_all | solution.py:16
  102.2 3.5 %collective-permute-start = (bf16[1,256,1024]{2,1,0:T(8,128)(2,1)S(1)}, bf16[1,256,1024]{2,1,0:T(8,128)(2,1)}, u32[]{:S(2)}, u32[]{:S(2)}) collective-permute-start(bf16[1,256,1024]{2,1,0:T(8,128)(2,1)S(1)} %copy-done.1), channel_id=1, source_target_pairs={{0,8},{8,16},{16,24},{24,32},{32,40},{40,48},{48,56},{56,64},{64,7... | collective-permute-start | bytes 1572872 | tf_op jit(solution)/shard_map/ppermute | solution.py:38
  105.7 1.7 fusion.7
  107.5 10.6 %all-to-all-done = f32[16,16,1024]{2,1,0:T(8,128)S(1)} async-done(((f32[16,16,1024]{2,1,0:T(8,128)}), f32[16,16,1024]{2,1,0:T(8,128)S(1)}, u32[]{:S(2)}, u32[]{:S(2)}) %all-to-all-start) | async-done | bytes 1048608 | tf_op jit(solution)/shard_map/all_to_all | solution.py:16
  118.0 0.1 reduce_sum.22
  118.1 0.9 convolution_convert_fusion.1
  119.0 0.9 broadcast_in_dim.2
  119.9 4.1 %all-to-all-start.1 = ((bf16[16,16,1024]{2,1,0:T(8,128)(2,1)}), bf16[16,16,1024]{2,1,0:T(8,128)(2,1)S(1)}, u32[]{:S(2)}, u32[]{:S(2)}) async-start(bf16[16,16,1024]{2,1,0:T(8,128)(2,1)} %broadcast_in_dim.2), calls=%async_computation.1 | async-start | bytes 1048576 | tf_op jit(solution)/shard_map/all_to_all | solution.py:28
  124.0 0.0 all-gather.5.cloned.1.call-start
  124.0 0.0 collective-permute-done
  124.0 9.9 %all-to-all-done.1 = bf16[16,16,1024]{2,1,0:T(8,128)(2,1)S(1)} async-done(((bf16[16,16,1024]{2,1,0:T(8,128)(2,1)}), bf16[16,16,1024]{2,1,0:T(8,128)(2,1)S(1)}, u32[]{:S(2)}, u32[]{:S(2)}) %all-to-all-start.1) | async-done | bytes 524320 | tf_op jit(solution)/shard_map/all_to_all | solution.py:28
  134.0 1.9 bitcast_select_fusion
  135.9 0.0 all-gather.5.cloned.1.call-update
  135.9 67.8 %all-gather.5.cloned.1.call-done = bf16[1,256,8192]{2,1,0:T(8,128)(2,1)} async-done(((bf16[1,256,1024]{2,1,0:T(8,128)(2,1)}), bf16[1,256,8192]{2,1,0:T(8,128)(2,1)}) %all-gather.5.cloned.1.call-update) | async-done | bytes 4194320 | tf_op jit(solution)/shard_map/all_gather | solution.py:65
  203.7 12.5 %fusion = f32[16,16,1024]{2,1,0:T(8,128)} fusion(bf16[16,16,8192]{2,1,0:T(8,128)(2,1)} %bitcast.43, bf16[1,1024,8192]{2,1,0:T(8,128)(2,1)} %param.4), kind=kOutput, calls=%fused_computation | convolution fusion | flops 4294967296 | bytes 22020096 | tf_op jit(solution)/shard_map/lrc,lkc->rk/dot_general | solution.py:63
  216.2 5.4 %all-to-all-start.2 = ((f32[16,16,1024]{2,1,0:T(8,128)}), f32[16,16,1024]{2,1,0:T(8,128)S(1)}, u32[]{:S(2)}, u32[]{:S(2)}) async-start(f32[16,16,1024]{2,1,0:T(8,128)} %fusion), calls=%async_computation.2 | async-start | bytes 2097152 | tf_op jit(solution)/shard_map/all_to_all | solution.py:16
  221.7 15.8 %all-to-all-done.2 = f32[16,16,1024]{2,1,0:T(8,128)S(1)} async-done(((f32[16,16,1024]{2,1,0:T(8,128)}), f32[16,16,1024]{2,1,0:T(8,128)S(1)}, u32[]{:S(2)}, u32[]{:S(2)}) %all-to-all-start.2) | async-done | bytes 1048608 | tf_op jit(solution)/shard_map/all_to_all | solution.py:16
  237.5 0.1 reduce_sum.24
  237.6 0.9 fusion.4
  238.6 0.6 pad_maximum_fusion
  (17 shorter events, 0.2 us)
Async XLA Ops:
  6.5 111.6 %copy-start = (f32[8,128,128]{2,1,0:T(8,128)S(1)}, f32[8,128,128]{2,1,0:T(8,128)}, u32[]{:S(2)}) copy-start(f32[8,128,128]{2,1,0:T(8,128)} %param.7) | copy-start | bytes 1572868
  6.5 77.6 %all-gather.3.cloned.1.call-start = ((), (), s32[]{:S(2)}) async-start(), calls=%async_computation.3 | async-start | bytes 4718592 | tf_op jit(solution)/shard_map/all_gather | solution.py:65
  84.2 18.0 %copy-start.1 = (bf16[1,256,1024]{2,1,0:T(8,128)(2,1)S(1)}, bf16[1,256,1024]{2,1,0:T(8,128)(2,1)}, u32[]{:S(2)}) copy-start(bf16[1,256,1024]{2,1,0:T(8,128)(2,1)} %param.5) | copy-start | bytes 1572868
  96.7 21.3 %all-to-all-start = ((f32[16,16,1024]{2,1,0:T(8,128)}), f32[16,16,1024]{2,1,0:T(8,128)S(1)}, u32[]{:S(2)}, u32[]{:S(2)}) async-start(f32[16,16,1024]{2,1,0:T(8,128)} %fusion.2), calls=%async_computation | async-start | bytes 2097152 | tf_op jit(solution)/shard_map/all_to_all | solution.py:16
  102.2 21.9 %collective-permute-start = (bf16[1,256,1024]{2,1,0:T(8,128)(2,1)S(1)}, bf16[1,256,1024]{2,1,0:T(8,128)(2,1)}, u32[]{:S(2)}, u32[]{:S(2)}) collective-permute-start(bf16[1,256,1024]{2,1,0:T(8,128)(2,1)S(1)} %copy-done.1), channel_id=1, source_target_pairs={{0,8},{8,16},{16,24},{24,32},{32,40},{40,48},{48,56},{56,64},{64,7... | collective-permute-start | bytes 1572872 | tf_op jit(solution)/shard_map/ppermute | solution.py:38
  119.9 14.1 %all-to-all-start.1 = ((bf16[16,16,1024]{2,1,0:T(8,128)(2,1)}), bf16[16,16,1024]{2,1,0:T(8,128)(2,1)S(1)}, u32[]{:S(2)}, u32[]{:S(2)}) async-start(bf16[16,16,1024]{2,1,0:T(8,128)(2,1)} %broadcast_in_dim.2), calls=%async_computation.1 | async-start | bytes 1048576 | tf_op jit(solution)/shard_map/all_to_all | solution.py:28
  124.0 79.7 %all-gather.5.cloned.1.call-start = ((), (), s32[]{:S(2)}) async-start(), calls=%async_computation.4 | async-start | bytes 4718592 | tf_op jit(solution)/shard_map/all_gather | solution.py:65
  216.2 21.3 %all-to-all-start.2 = ((f32[16,16,1024]{2,1,0:T(8,128)}), f32[16,16,1024]{2,1,0:T(8,128)S(1)}, u32[]{:S(2)}, u32[]{:S(2)}) async-start(f32[16,16,1024]{2,1,0:T(8,128)} %fusion), calls=%async_computation.2 | async-start | bytes 2097152 | tf_op jit(solution)/shard_map/all_to_all | solution.py:16
Sparse Core Ops, SparseCore 0:
  9.7 74.3 all-gather.2
  136.0 67.6 all-gather.4
where the time goes:
time: 247 us; the launch traced here: 246 us
  waiting for transfers between devices  182 us (74%)
  matrix products  26.9 us (11%)
  starting transfers between devices  18.5 us (7%)
  between operations  13.5 us (5%)
  local copies, waits for them, and re-layouts  2.71 us (1%)
  other arithmetic  2.68 us (1%)
    all_gather x2, waiting for transfers between devices, per_device(): lax.all_gather(current_loc, 'row', axis=2, tiled=True)  145 us
    all_to_all x2, waiting for transfers between devices, summed_on_arrival(): lax.all_to_all(tiles, axis, split_axis=0, concat_axis=0, tiled=True)  26.3 us
    dot_general x2, matrix products, per_device(): jnp.einsum('lrc,lkc->rk', lax.all_gather(current_loc, 'row', axis=2, tile...  25.1 us
    all_to_all x2, starting transfers between devices, summed_on_arrival(): lax.all_to_all(tiles, axis, split_axis=0, concat_axis=0, tiled=True)  10.9 us
    all_to_all x1, waiting for transfers between devices, from_everyone(): lax.all_to_all(jnp.broadcast_to(x[None], (peers, *x.shape)), axis, 0, 0,...  9.92 us
  transfers between devices with their start and end apart: 6, of which 5 were waited for; matrix products, arithmetic and copies ran while one was open for 1% of the time, Pallas kernels for 0%

commit v1 on v0

--- a/solution.py
+++ b/solution.py
@@ -1,9 +1,19 @@
+import functools
 import jax
 import jax.numpy as jnp
 from jax import lax
 from jax.sharding import PartitionSpec as P
 
 STEPS = 2
+
+
+def balance_shelves_on(packet, ax_name):
+    return jnp.concatenate(
+        lax.all_to_all(jnp.stack(lax.psum(1, ax_name) * [packet], 0), ax_name, 0, 0), 2
+    )
+
+
+body_balance = functools.partial(balance_shelves_on, ax_name="row")
 
 
 def in_blocks(x, dim, peers):
@@ -61,10 +71,7 @@
     results = []
     for step in range(STEPS):
         partial_value = jnp.einsum(
-            "lrc,lkc->rk",
-            lax.all_gather(current_loc, "row", axis=2, tiled=True),
-            lag_matrix,
-            preferred_element_type=jnp.float32,
+            "lrc,lkc->rk", body_balance(current_loc), lag_matrix, preferred_element_type=jnp.float32
         )
         history = summed_on_arrival(partial_value, "lag", 0)
         mine = lax.dynamic_slice_in_dim(excitation[step], offset, share, 0)

time: 247 us -> 225 us (0.911)
  waiting for transfers between devices: 182 us -> 36.4 us
  blocking collectives: 0 us -> 111 us
  local copies, waits for them, and re-layouts: 2.71 us -> 28.2 us
  between operations: 13.5 us -> 0.16 us
    all_gather x2 -> x0, waiting for transfers between devices: 145 us -> none  [per_device(): lax.all_gather(current_loc, 'row', axis=2, tiled=True)]
    all_to_all x0 -> x2, blocking collectives: none -> 111 us  [balance_shelves_on(): lax.all_to_all(jnp.stack(lax.psum(1, ax_name) * [packet], 0), ax_name, 0, 0)]
    dot_general x0 -> x2, local copies, waits for them, and re-layouts: none -> 14.8 us  [per_device(): jnp.einsum('lrc,lkc->rk', body_balance(current_loc), lag_matrix, preferre...]
    reshape x0 -> x2, local copies, waits for them, and re-layouts: none -> 8.58 us  [balance_shelves_on(): jnp.concatenate(lax.all_to_all(jnp.stack(lax.psum(1, ax_name) * [packet],...]
  transfers between devices with their start and end apart: 6 -> 4, of which waited for: 5 -> 3; matrix products, arithmetic and copies ran while one was open for 1% -> 2% of each run, Pallas kernels for 0% -> 0%
where the time goes in v1:
time: 225 us; the launch traced here: 224 us
  blocking collectives  111 us (49%)
  waiting for transfers between devices  36.4 us (16%)
  local copies, waits for them, and re-layouts  28.2 us (13%)
  matrix products  27 us (12%)
  starting transfers between devices  19.5 us (9%)
    all_to_all x2, blocking collectives, balance_shelves_on(): lax.all_to_all(jnp.stack(lax.psum(1, ax_name) * [packet], 0), ax_name, 0, 0)  111 us
    all_to_all x2, waiting for transfers between devices, summed_on_arrival(): lax.all_to_all(tiles, axis, split_axis=0, concat_axis=0, tiled=True)  26.4 us
    dot_general x2, matrix products, per_device(): jnp.einsum('lrc,lkc->rk', body_balance(current_loc), lag_matrix, preferre...  25.1 us
    dot_general x2, local copies, waits for them, and re-layouts, per_device(): jnp.einsum('lrc,lkc->rk', body_balance(current_loc), lag_matrix, preferre...  14.8 us
    all_to_all x2, starting transfers between devices, summed_on_arrival(): lax.all_to_all(tiles, axis, split_axis=0, concat_axis=0, tiled=True)  11.9 us
    all_to_all x1, waiting for transfers between devices, from_everyone(): lax.all_to_all(jnp.broadcast_to(x[None], (peers, *x.shape)), axis, 0, 0,...  9.98 us
    reshape x2, local copies, waits for them, and re-layouts, balance_shelves_on(): jnp.concatenate(lax.all_to_all(jnp.stack(lax.psum(1, ax_name) * [packet],...  8.58 us
  transfers between devices with their start and end apart: 4, of which 3 were waited for; matrix products, arithmetic and copies ran while one was open for 2% of the time, Pallas kernels for 0%

profile of v1, /device:TPU:1, one launch (start us, length us, event | category | flops | bytes accessed | tf_op | source)
XLA Modules:
  0.0 224.4 jit_solution(11821504928805476751)
XLA Ops:
  0.0 1.6 stack.6
  1.6 57.3 %all_to_all.25 = bf16[8,1,256,1024]{3,2,1,0:T(8,128)(2,1)S(1)} all-to-all(bf16[8,1,256,1024]{3,2,1,0:T(8,128)(2,1)S(1)} %stack.6), channel_id=1, replica_groups=mesh['lag'=16,'row'=8] {'row'}, dimensions={0} | all-to-all | bytes 8388608 | tf_op jit(solution)/shard_map/all_to_all | solution.py:12
  59.0 4.3 %copy.10 = bf16[1,256,8,1024]{3,2,1,0:T(8,128)(2,1)} copy(bf16[1,256,8,1024]{3,1,0,2:T(8,128)(2,1)S(1)} %bitcast.48) | data formatting | bytes 8388608 | tf_op jit(solution)/shard_map/reshape | solution.py:11
  63.3 7.4 %dot_general.16 = bf16[16,16,8192]{2,1,0:T(8,128)(2,1)} reshape(bf16[1,256,8,1024]{3,2,1,0:T(8,128)(2,1)} %copy.10) | data formatting | bytes 8388608 | tf_op jit(solution)/shard_map/lrc,lkc->rk/dot_general | solution.py:73
  70.7 12.6 %fusion.2 = f32[16,16,1024]{2,1,0:T(8,128)} fusion(bf16[16,16,8192]{2,1,0:T(8,128)(2,1)} %dot_general.16, bf16[1,1024,8192]{2,1,0:T(8,128)(2,1)} %param.4), kind=kOutput, calls=%fused_computation.2 | convolution fusion | flops 4294967296 | bytes 22020096 | tf_op jit(solution)/shard_map/lrc,lkc->rk/dot_general | solution.py:73
  83.2 7.3 %all-to-all-start.1 = ((f32[16,16,1024]{2,1,0:T(8,128)}), f32[16,16,1024]{2,1,0:T(8,128)S(1)}, u32[]{:S(2)}, u32[]{:S(2)}) async-start(f32[16,16,1024]{2,1,0:T(8,128)} %fusion.2), calls=%async_computation.1 | async-start | bytes 2097152 | tf_op jit(solution)/shard_map/all_to_all | solution.py:26
  90.5 3.5 %collective-permute-start = (bf16[1,256,1024]{2,1,0:T(8,128)(2,1)S(1)}, bf16[1,256,1024]{2,1,0:T(8,128)(2,1)}, u32[]{:S(2)}, u32[]{:S(2)}) collective-permute-start(bf16[1,256,1024]{2,1,0:T(8,128)(2,1)S(1)} %copy-done.1), channel_id=1, source_target_pairs={{0,8},{8,16},{16,24},{24,32},{32,40},{40,48},{48,56},{56,64},{64,7... | collective-permute-start | bytes 1572872 | tf_op jit(solution)/shard_map/ppermute | solution.py:48
  94.1 1.7 fusion.8
  95.8 10.6 %all-to-all-done.1 = f32[16,16,1024]{2,1,0:T(8,128)S(1)} async-done(((f32[16,16,1024]{2,1,0:T(8,128)}), f32[16,16,1024]{2,1,0:T(8,128)S(1)}, u32[]{:S(2)}, u32[]{:S(2)}) %all-to-all-start.1) | async-done | bytes 1048608 | tf_op jit(solution)/shard_map/all_to_all | solution.py:26
  106.4 0.1 reduce_sum.22
  106.5 0.9 convolution_convert_fusion.1
  107.4 0.9 broadcast_in_dim.2
  108.3 4.1 %all-to-all-start.2 = ((bf16[16,16,1024]{2,1,0:T(8,128)(2,1)}), bf16[16,16,1024]{2,1,0:T(8,128)(2,1)S(1)}, u32[]{:S(2)}, u32[]{:S(2)}) async-start(bf16[16,16,1024]{2,1,0:T(8,128)(2,1)} %broadcast_in_dim.2), calls=%async_computation.2 | async-start | bytes 1048576 | tf_op jit(solution)/shard_map/all_to_all | solution.py:38
  112.4 10.0 %all-to-all-done.2 = bf16[16,16,1024]{2,1,0:T(8,128)(2,1)S(1)} async-done(((bf16[16,16,1024]{2,1,0:T(8,128)(2,1)}), bf16[16,16,1024]{2,1,0:T(8,128)(2,1)S(1)}, u32[]{:S(2)}, u32[]{:S(2)}) %all-to-all-start.2) | async-done | bytes 524320 | tf_op jit(solution)/shard_map/all_to_all | solution.py:38
  122.3 1.1 fusion.5
  123.4 0.5 stack.7
  124.0 54.0 %all_to_all.26 = bf16[8,1,256,1024]{3,2,1,0:T(8,128)(2,1)S(1)} all-to-all(bf16[8,1,256,1024]{3,2,1,0:T(8,128)(2,1)S(1)} %stack.7), channel_id=1, replica_groups=mesh['lag'=16,'row'=8] {'row'}, dimensions={0} | all-to-all | bytes 8388608 | tf_op jit(solution)/shard_map/all_to_all | solution.py:12
  178.0 4.3 %copy.14 = bf16[1,256,8,1024]{3,2,1,0:T(8,128)(2,1)} copy(bf16[1,256,8,1024]{3,1,0,2:T(8,128)(2,1)S(1)} %bitcast.49) | data formatting | bytes 8388608 | tf_op jit(solution)/shard_map/reshape | solution.py:11
  182.3 7.4 %dot_general.19 = bf16[16,16,8192]{2,1,0:T(8,128)(2,1)} reshape(bf16[1,256,8,1024]{3,2,1,0:T(8,128)(2,1)} %copy.14) | data formatting | bytes 8388608 | tf_op jit(solution)/shard_map/lrc,lkc->rk/dot_general | solution.py:73
  189.6 12.5 %fusion = f32[16,16,1024]{2,1,0:T(8,128)} fusion(bf16[16,16,8192]{2,1,0:T(8,128)(2,1)} %dot_general.19, bf16[1,1024,8192]{2,1,0:T(8,128)(2,1)} %param.4), kind=kOutput, calls=%fused_computation | convolution fusion | flops 4294967296 | bytes 22020096 | tf_op jit(solution)/shard_map/lrc,lkc->rk/dot_general | solution.py:73
  202.2 4.6 %all-to-all-start.4 = ((f32[16,16,1024]{2,1,0:T(8,128)}), f32[16,16,1024]{2,1,0:T(8,128)S(1)}, u32[]{:S(2)}, u32[]{:S(2)}) async-start(f32[16,16,1024]{2,1,0:T(8,128)} %fusion), calls=%async_computation.4 | async-start | bytes 2097152 | tf_op jit(solution)/shard_map/all_to_all | solution.py:26
  206.8 15.9 %all-to-all-done.4 = f32[16,16,1024]{2,1,0:T(8,128)S(1)} async-done(((f32[16,16,1024]{2,1,0:T(8,128)}), f32[16,16,1024]{2,1,0:T(8,128)S(1)}, u32[]{:S(2)}, u32[]{:S(2)}) %all-to-all-start.4) | async-done | bytes 1048608 | tf_op jit(solution)/shard_map/all_to_all | solution.py:26
  222.8 0.9 fusion.4
  223.8 0.6 pad_maximum_fusion
  (19 shorter events, 0.2 us)
Async XLA Ops:
  0.0 106.5 %copy-start = (f32[8,128,128]{2,1,0:T(8,128)S(1)}, f32[8,128,128]{2,1,0:T(8,128)}, u32[]{:S(2)}) copy-start(f32[8,128,128]{2,1,0:T(8,128)} %param.7) | copy-start | bytes 1572868
  70.7 19.9 %copy-start.1 = (bf16[1,256,1024]{2,1,0:T(8,128)(2,1)S(1)}, bf16[1,256,1024]{2,1,0:T(8,128)(2,1)}, u32[]{:S(2)}) copy-start(bf16[1,256,1024]{2,1,0:T(8,128)(2,1)} %param.5) | copy-start | bytes 1572868
  83.2 23.1 %all-to-all-start.1 = ((f32[16,16,1024]{2,1,0:T(8,128)}), f32[16,16,1024]{2,1,0:T(8,128)S(1)}, u32[]{:S(2)}, u32[]{:S(2)}) async-start(f32[16,16,1024]{2,1,0:T(8,128)} %fusion.2), calls=%async_computation.1 | async-start | bytes 2097152 | tf_op jit(solution)/shard_map/all_to_all | solution.py:26
  90.5 21.8 %collective-permute-start = (bf16[1,256,1024]{2,1,0:T(8,128)(2,1)S(1)}, bf16[1,256,1024]{2,1,0:T(8,128)(2,1)}, u32[]{:S(2)}, u32[]{:S(2)}) collective-permute-start(bf16[1,256,1024]{2,1,0:T(8,128)(2,1)S(1)} %copy-done.1), channel_id=1, source_target_pairs={{0,8},{8,16},{16,24},{24,32},{32,40},{40,48},{48,56},{56,64},{64,7... | collective-permute-start | bytes 1572872 | tf_op jit(solution)/shard_map/ppermute | solution.py:48
  108.3 14.1 %all-to-all-start.2 = ((bf16[16,16,1024]{2,1,0:T(8,128)(2,1)}), bf16[16,16,1024]{2,1,0:T(8,128)(2,1)S(1)}, u32[]{:S(2)}, u32[]{:S(2)}) async-start(bf16[16,16,1024]{2,1,0:T(8,128)(2,1)} %broadcast_in_dim.2), calls=%async_computation.2 | async-start | bytes 1048576 | tf_op jit(solution)/shard_map/all_to_all | solution.py:38
  202.2 20.5 %all-to-all-start.4 = ((f32[16,16,1024]{2,1,0:T(8,128)}), f32[16,16,1024]{2,1,0:T(8,128)S(1)}, u32[]{:S(2)}, u32[]{:S(2)}) async-start(f32[16,16,1024]{2,1,0:T(8,128)} %fusion), calls=%async_computation.4 | async-start | bytes 2097152 | tf_op jit(solution)/shard_map/all_to_all | solution.py:26
